TPU v7x, 256 devices: a whole 4x4x8 slice. The times are simulated.
256 devices in a mesh: batch: 8 (over z), col: 32 (over y, x, core).
Axes of the slice: x: 4, y: 4, z: 8, core: 2. Of those that a mesh axis runs over, the one named last changes fastest.
Arguments:
- views: bfloat16 [2, 1024, 4096], P(None, 'batch', 'col'), may hold values from -132 to 132
- norm_scale_gain: float32 [4096], P('col'), may hold values from 0.5 to 1.5
- norm_shift_bias: float32 [4096], P('col'), may hold values from -3 to 3
- weight: bfloat16 [4096, 8192], P(None, 'col'), may hold values from -0.09375 to 0.09375
Outputs:
- loss: float32 [], replicated
- grad_weight: float32 [4096, 8192], P('batch', 'col')
- grad_gain: float32 [4096], P('col')
- grad_bias: float32 [4096], P('col')
- views_gradient: float32 [2, 1024, 4096], P(None, 'batch', 'col')
All inputs are finite; a program needn't handle non-finite values.
Results may differ from a plain program's by a relative error of at most 0.0027.
Values may be sent and summed in bfloat16 or wider, within the bound.
A program may use at most 64 MiB of HBM per device.

v0:
```python
import jax
import jax.numpy as jnp
from jax import lax
from jax.sharding import PartitionSpec as P

E = 8192
eps_norm = 1e-05
eps_std = 0.0001


def gelu_slope(preactivation):
    value, pullback = jax.vjp(lambda t: jax.nn.gelu(t, approximate=True), preactivation)
    return pullback(jnp.ones_like(value))[0]


def shards(views, norm_scale_gain, norm_shift_bias, weight):
    n_batch = lax.axis_size("batch")
    n_col = lax.axis_size("col")
    local_rows = views.shape[1]
    sample_count = local_rows * n_batch
    scale = sample_count * E / 128.0
    hidden_float = views.astype(jnp.float32)
    total = lax.psum(jnp.sum(hidden_float, axis=1), "batch")
    batch_average = total[:, None, :] / sample_count
    centred = hidden_float - batch_average
    spread = lax.psum(jnp.sum(centred * centred, axis=1), "batch")
    var = spread[:, None, :] / sample_count
    inverse_deviation = 1.0 / jnp.sqrt(var + eps_norm)
    normalised_input = (hidden_float - batch_average) * inverse_deviation
    preactivation = norm_scale_gain * normalised_input + norm_shift_bias
    act = jax.nn.gelu(preactivation, approximate=True).astype(jnp.bfloat16)
    act_full = lax.all_gather(act, "col", axis=2, tiled=True)
    z_local = jnp.einsum(
        "vrk,kj->vrj", act_full, weight, preferred_element_type=jnp.float32
    ).astype(jnp.bfloat16)
    z_all = lax.all_gather(z_local, "batch", axis=1, tiled=True)
    zf_all = z_all.astype(jnp.float32)
    zmean = jnp.mean(zf_all, axis=1, keepdims=True)
    zc_all = zf_all - zmean
    zvar = jnp.sum(zc_all * zc_all, axis=1, keepdims=True) / (sample_count - 1)
    std = jnp.sqrt(zvar + eps_std)
    zcb_all = zc_all.astype(jnp.bfloat16)
    offset = lax.axis_index("batch") * local_rows
    zc_loc = lax.dynamic_slice_in_dim(zc_all, offset, local_rows, 1)
    zcb_loc = zc_loc.astype(jnp.bfloat16)
    diag = jnp.sum(jnp.square(zcb_all.astype(jnp.float32)), axis=1, keepdims=True)
    kernel_part = jnp.einsum("vrj,vmj->vrm", zcb_loc, zcb_all, preferred_element_type=jnp.float32)
    kernel = lax.psum(kernel_part, "col")
    kernel_b = kernel.astype(jnp.bfloat16)
    denom = float((sample_count - 1) ** 2 * E)
    coef = 4.0 * scale / denom
    hinge_coef = 25.0 * scale / (2.0 * E * (sample_count - 1))
    mask = jnp.where(std < 1.0, 1.0, 0.0)
    moved = jnp.einsum("vrm,vmj->vrj", kernel_b, zcb_all, preferred_element_type=jnp.float32)
    g_cov = coef * (moved - zcb_loc.astype(jnp.float32) * diag)
    g_var = -hinge_coef * mask * zc_loc / std
    summed = g_cov + g_var
    col_total = lax.psum(jnp.sum(summed, axis=1), "batch")
    zf_loc = z_local.astype(jnp.float32)
    diff = zf_loc[0] - zf_loc[1]
    g_inv = 50.0 * scale / (sample_count * E) * diff
    dz = summed - col_total[:, None, :] / sample_count + jnp.stack([g_inv, -g_inv])
    dzb = dz.astype(jnp.bfloat16)
    inv_share = jnp.sum(diff * diff) / (sample_count * E)
    hinge_share = jnp.sum(jnp.maximum(1.0 - std, 0.0)) / (2 * E)
    block_share = jnp.sum(kernel * kernel) / denom
    diag_share = jnp.sum(diag * diag) / denom
    share = 25.0 * inv_share + (25.0 * hinge_share - diag_share) / n_batch + block_share / n_col
    loss = lax.psum(share, ("batch", "col"))
    d_act_t = lax.psum_scatter(
        jnp.einsum("kj,vrj->kvr", weight, dzb, preferred_element_type=jnp.float32),
        "col",
        scatter_dimension=0,
        tiled=True,
    )
    d_act = jnp.transpose(d_act_t, (1, 2, 0))
    grad_weight = lax.psum_scatter(
        jnp.einsum("vrk,vrj->kj", act_full, dzb, preferred_element_type=jnp.float32),
        "batch",
        scatter_dimension=0,
        tiled=True,
    )
    preactivation_gradient = d_act * gelu_slope(preactivation)
    bias_gradient_sum, gain_gradient_sum = lax.psum(
        (
            jnp.sum(preactivation_gradient, axis=1),
            jnp.sum(preactivation_gradient * normalised_input, axis=1),
        ),
        "batch",
    )
    grad_bias = jnp.sum(bias_gradient_sum, axis=0)
    grad_gain = jnp.sum(gain_gradient_sum, axis=0)
    views_gradient = (
        norm_scale_gain
        * (
            preactivation_gradient
            - bias_gradient_sum[:, None, :] / sample_count
            - normalised_input * gain_gradient_sum[:, None, :] / sample_count
        )
        * inverse_deviation
    )
    return (loss, grad_weight, grad_gain, grad_bias, views_gradient)


def solution(mesh):
    placed = (P(None, "batch", "col"), P("col"), P("col"), P(None, "col"))
    return jax.shard_map(
        shards,
        mesh=mesh,
        in_specs=placed,
        out_specs=(P(), P("batch", "col"), P("col"), P("col"), P(None, "batch", "col")),
        check_vma=False,
    )
```

profile of v0, /device:TPU:1, one launch (start us, length us, event | category | flops | bytes accessed | tf_op | source)
XLA Modules:
  0.0 430.3 jit_solution(8545685748164966906)
XLA Ops:
  7.2 1.0 convert_reduce_fusion.1
  8.2 17.3 %psum.49 = f32[2,128]{1,0:T(2,128)S(1)} all-reduce(f32[2,128]{1,0:T(2,128)S(1)} %convert_reduce_fusion.1), channel_id=1, replica_groups=mesh['batch'=8,'col'=32] {'batch'}, use_global_device_ids=true, to_apply=%region_1.0 | all-reduce | flops 256 | bytes 2048 | tf_op jit(solution)/shard_map/psum | solution.py:23
  26.4 10.8 %psum.50 = f32[2,128]{1,0:T(2,128)S(1)} all-reduce(f32[2,128]{1,0:T(2,128)S(1)} %fusion.32), channel_id=1, replica_groups=mesh['batch'=8,'col'=32] {'batch'}, use_global_device_ids=true, to_apply=%region_3.0 | all-reduce | flops 256 | bytes 2048 | tf_op jit(solution)/shard_map/psum | solution.py:26
  37.2 1.6 fusion.25
  38.8 56.4 %all-gather.3.cloned.1.call-done = bf16[2,128,4096]{2,1,0:T(8,128)(2,1)} async-done(((bf16[2,128,128]{2,1,0:T(8,128)(2,1)}), bf16[2,128,4096]{2,1,0:T(8,128)(2,1)}) %all-gather.3.cloned.1.call-update) | async-done | bytes 2097168 | tf_op jit(solution)/shard_map/all_gather | solution.py:32
  95.2 3.0 fusion.42
  98.2 32.8 %all-gather.5.cloned.1.call-done = bf16[2,1024,256]{2,1,0:T(8,128)(2,1)} async-done(((bf16[2,128,256]{2,1,0:T(8,128)(2,1)}), bf16[2,1024,256]{2,1,0:T(8,128)(2,1)}) %all-gather.5.cloned.1.call-update) | async-done | bytes 1048592 | tf_op jit(solution)/shard_map/all_gather | solution.py:36
  131.1 1.5 convert_reduce_fusion
  132.6 2.1 multiply_reduce_fusion
  134.7 1.3 copy-done.2
  136.0 1.5 fusion.10
  137.6 1.3 fusion.41
  138.8 1.3 fusion.37
  140.2 115.7 %all-reduce.3.cloned.1.call-done = f32[2,128,1024]{2,1,0:T(8,128)} async-done(((f32[2,128,1024]{2,1,0:T(8,128)}), f32[2,128,1024]{2,1,0:T(8,128)}) %all-reduce.3.cloned.1.call-update) | async-done | bytes 1048592 | tf_op jit(solution)/shard_map/psum | solution.py:48
  255.9 2.4 fusion.43
  258.3 13.7 %psum.53 = f32[2,256]{1,0:T(2,128)S(1)} all-reduce(f32[2,256]{1,0:T(2,128)S(1)} %get-tuple-element.23), channel_id=1, replica_groups=mesh['batch'=8,'col'=32] {'batch'}, use_global_device_ids=true, to_apply=%region_14.15 | all-reduce | flops 512 | bytes 4096 | tf_op jit(solution)/shard_map/psum | solution.py:58
  272.0 1.0 fusion.13
  272.9 2.7 convolution_bitcast_fusion
  275.7 4.3 convolution_bitcast_fusion.1
  284.2 78.4 %psum.52 = f32[]{:T(128)} all-reduce(f32[]{:T(128)S(6)} %add.83), channel_id=1, replica_groups=mesh['batch'=8,'col'=32] {'batch','col'}, use_global_device_ids=true, to_apply=%region_12.13 | all-reduce | flops 1 | bytes 8 | tf_op jit(solution)/shard_map/psum | solution.py:69
  362.6 1.7 reduce-scatter.5.cloned.1.call-done
  364.4 1.0 fusion.39
  365.4 14.1 %all-reduce = (f32[2,128]{1,0:T(2,128)S(1)}, f32[2,128]{1,0:T(2,128)S(1)}) all-reduce(f32[2,128]{1,0:T(2,128)S(1)} %get-tuple-element.8, f32[2,128]{1,0:T(2,128)S(1)} %get-tuple-element.7), channel_id=1, replica_groups=mesh['batch'=8,'col'=32] {'batch'}, use_global_device_ids=true, to_apply=%region_18.19 | all-reduce | flops 512 | bytes 4096 | tf_op jit(solution)/shard_map/psum | solution.py:84
  381.3 42.5 %reduce-scatter.3.cloned.1.call-done = f32[512,256]{1,0:T(8,128)} async-done(((f32[4096,256]{1,0:T(8,128)}), f32[512,256]{1,0:T(8,128)}) %reduce-scatter.3.cloned.1.call-update) | async-done | bytes 524304 | tf_op jit(solution)/shard_map/reduce_scatter | solution.py:77
  (35 shorter events, 4.5 us)
Async XLA Ops:
  7.2 88.0 %copy-start = (bf16[4096,256]{1,0:T(8,128)(2,1)S(1)}, bf16[4096,256]{1,0:T(8,128)(2,1)}, u32[]{:S(2)}) copy-start(bf16[4096,256]{1,0:T(8,128)(2,1)} %param.7) | copy-start | bytes 6291460
  7.2 88.0 %all-gather.3.cloned.1.call-start = ((), (), s32[]{:S(2)}) async-start(), calls=%async_computation.2 | async-start | bytes 2162688 | tf_op jit(solution)/shard_map/all_gather | solution.py:32
  38.8 92.3 %all-gather.5.cloned.1.call-start = ((), (), s32[]{:S(2)}) async-start(), calls=%async_computation.3 | async-start | bytes 1179648 | tf_op jit(solution)/shard_map/all_gather | solution.py:36
  98.2 157.7 %all-reduce.3.cloned.1.call-start = ((), (), s32[]{:S(2)}) async-start(), calls=%async_computation.4 | async-start | bytes 2097152 | tf_op jit(solution)/shard_map/psum | solution.py:48
  131.1 5.0 %copy-start.1 = (bf16[2,1024,256]{2,1,0:T(8,128)(2,1)S(1)}, bf16[2,1024,256]{2,1,0:T(8,128)(2,1)}, u32[]{:S(2)}) copy-start(bf16[2,1024,256]{2,1,0:T(8,128)(2,1)} %all-gather.5.cloned.1.call-done) | copy-start | bytes 3145732
  134.6 1.4 copy-start.2
  137.5 226.9 %reduce-scatter.5.cloned.1.call-start = ((), (), s32[]{:S(2)}) async-start(), calls=%async_computation.6 | async-start | bytes 4325376 | tf_op jit(solution)/shard_map/reduce_scatter | solution.py:70
  138.8 133.1 %copy-start.5 = (f32[1,128,256]{2,1,0:T(8,128)S(1)}, f32[1,128,256]{2,1,0:T(8,128)}, u32[]{:S(2)}) copy-start(f32[1,128,256]{2,1,0:T(8,128)} %get-tuple-element.13) | copy-start | bytes 393220
  275.7 148.1 %reduce-scatter.3.cloned.1.call-start = ((), (), s32[]{:S(2)}) async-start(), calls=%async_computation.5 | async-start | bytes 4718592 | tf_op jit(solution)/shard_map/reduce_scatter | solution.py:77
  280.0 2.7 copy-start.4
  280.0 84.3 %copy-start.3 = (bf16[2,128,128]{2,1,0:T(8,128)(2,1)S(1)}, bf16[2,128,128]{2,1,0:T(8,128)(2,1)}, u32[]{:S(2)}) copy-start(bf16[2,128,128]{2,1,0:T(8,128)(2,1)} %param.4) | copy-start | bytes 196612
  280.0 84.3 %copy-start.6 = (f32[128]{0:T(128)S(1)}, f32[128]{0:T(128)}, u32[]{:S(2)}) copy-start(f32[128]{0:T(128)} %param.5) | copy-start | bytes 1540
  280.0 84.3 %copy-start.7 = (f32[128]{0:T(128)S(1)}, f32[128]{0:T(128)}, u32[]{:S(2)}) copy-start(f32[128]{0:T(128)} %param.6) | copy-start | bytes 1540
Sparse Core Ops, SparseCore 0:
  38.9 56.2 all-gather.2
  98.3 32.7 all-gather.4
  137.6 118.2 all-reduce.2
  275.8 88.5 reduce-scatter.4
  367.3 56.3 reduce-scatter.2
where the time goes:
time: 431 us; the launch traced here: 430 us
  waiting for transfers between devices  249 us (58%)
  blocking collectives  134 us (31%)
  between operations  16.5 us (4%)
  other arithmetic  14.9 us (3%)
  matrix products  13.8 us (3%)
    psum x1, waiting for transfers between devices, shards(): kernel = lax.psum(kernel_part, 'col')  116 us
    psum x1, blocking collectives, shards(): loss = lax.psum(share, ('batch', 'col'))  78.4 us
    all_gather x1, waiting for transfers between devices, shards(): act_full = lax.all_gather(act, 'col', axis=2, tiled=True)  56.4 us
    reduce_scatter x1, waiting for transfers between devices, shards(): lax.psum_scatter(jnp.einsum('vrk,vrj->kj', act_full, dzb, preferred_eleme...  42.5 us
    all_gather x1, waiting for transfers between devices, shards(): z_all = lax.all_gather(z_local, 'batch', axis=1, tiled=True)  32.8 us
    psum x1, blocking collectives, shards(): total = lax.psum(jnp.sum(hidden_float, axis=1), 'batch')  17.3 us
    psum x1, blocking collectives, shards(): lax.psum((jnp.sum(preactivation_gradient, axis=1), jnp.sum(preactivation_...  14.1 us
    psum x1, blocking collectives, shards(): col_total = lax.psum(jnp.sum(summed, axis=1), 'batch')  13.7 us
  transfers between devices with their start and end apart: 5, of which 5 were waited for; matrix products, arithmetic and copies ran while one was open for 3% of the time, Pallas kernels for 0%

commit v1 on v0

--- a/solution.py
+++ b/solution.py
@@ -33,7 +33,14 @@
     z_local = jnp.einsum(
         "vrk,kj->vrj", act_full, weight, preferred_element_type=jnp.float32
     ).astype(jnp.bfloat16)
-    z_all = lax.all_gather(z_local, "batch", axis=1, tiled=True)
+    ring = [z_local]
+    for hop in range(7):
+        ring.append(lax.ppermute(ring[-1], "batch", [(dev, (dev + 1) % 8) for dev in range(8)]))
+    z_all = jnp.roll(
+        jnp.concatenate(ring[::-1], axis=1),
+        (lax.axis_index("batch") + 1) * ring[0].shape[1],
+        axis=1,
+    )
     zf_all = z_all.astype(jnp.float32)
     zmean = jnp.mean(zf_all, axis=1, keepdims=True)
     zc_all = zf_all - zmean

time: 431 us -> 435 us (level)
  waiting for transfers between devices: 249 us -> 259 us
  other arithmetic: 14.9 us -> 9.55 us
    ppermute x0 -> x7, waiting for transfers between devices: none -> 38.1 us  [shards(): lax.ppermute(ring[-1], 'batch', [(dev, (dev + 1) % 8) for dev in range(8)])]
    all_gather x1 -> x0, waiting for transfers between devices: 32.8 us -> none  [shards(): z_all = lax.all_gather(z_local, 'batch', axis=1, tiled=True)]
  transfers between devices with their start and end apart: 5 -> 11, of which waited for: 5 -> 11; matrix products, arithmetic and copies ran while one was open for 3% -> 2% of each run, Pallas kernels for 0% -> 0%
where the time goes in v1:
time: 435 us
  waiting for transfers between devices  259 us (60%)
  blocking collectives  134 us (31%)
  between operations  16.7 us (4%)
  matrix products  12.7 us (3%)
  other arithmetic  9.55 us (2%)
    psum x1, waiting for transfers between devices, shards(): kernel = lax.psum(kernel_part, 'col')  119 us
    psum x1, blocking collectives, shards(): loss = lax.psum(share, ('batch', 'col'))  78.4 us
    all_gather x1, waiting for transfers between devices, shards(): act_full = lax.all_gather(act, 'col', axis=2, tiled=True)  56.4 us
    reduce_scatter x1, waiting for transfers between devices, shards(): lax.psum_scatter(jnp.einsum('vrk,vrj->kj', act_full, dzb, preferred_eleme...  42.9 us
    ppermute x7, waiting for transfers between devices, shards(): lax.ppermute(ring[-1], 'batch', [(dev, (dev + 1) % 8) for dev in range(8)])  38.1 us
    psum x1, blocking collectives, shards(): total = lax.psum(jnp.sum(hidden_float, axis=1), 'batch')  17.3 us
    psum x1, blocking collectives, shards(): col_total = lax.psum(jnp.sum(summed, axis=1), 'batch')  13.7 us
    psum x1, blocking collectives, shards(): lax.psum((jnp.sum(preactivation_gradient, axis=1), jnp.sum(preactivation_...  13.4 us
  transfers between devices with their start and end apart: 11, of which 11 were waited for; matrix products, arithmetic and copies ran while one was open for 2% of the time, Pallas kernels for 0%

profile of v1, /device:TPU:1, one launch (start us, length us, event | category | flops | bytes accessed | tf_op | source)
XLA Modules:
  0.0 434.6 jit_solution(4146744639509498059)
XLA Ops:
  8.2 17.3 %psum.49 = f32[2,128]{1,0:T(2,128)S(1)} all-reduce(f32[2,128]{1,0:T(2,128)S(1)} %convert_reduce_fusion.1), channel_id=1, replica_groups=mesh['batch'=8,'col'=32] {'batch'}, use_global_device_ids=true, to_apply=%region_1.0 | all-reduce | flops 256 | bytes 2048 | tf_op jit(solution)/shard_map/psum | solution.py:23
  26.4 10.8 %psum.50 = f32[2,128]{1,0:T(2,128)S(1)} all-reduce(f32[2,128]{1,0:T(2,128)S(1)} %fusion.32), channel_id=1, replica_groups=mesh['batch'=8,'col'=32] {'batch'}, use_global_device_ids=true, to_apply=%region_3.0 | all-reduce | flops 256 | bytes 2048 | tf_op jit(solution)/shard_map/psum | solution.py:26
  37.2 1.6 fusion.25
  38.8 56.4 %all-gather.2.cloned.1.call-done = bf16[2,128,4096]{2,1,0:T(8,128)(2,1)} async-done(((bf16[2,128,128]{2,1,0:T(8,128)(2,1)}), bf16[2,128,4096]{2,1,0:T(8,128)(2,1)}) %all-gather.2.cloned.1.call-update) | async-done | bytes 2097168 | tf_op jit(solution)/shard_map/all_gather | solution.py:32
  95.2 2.3 fusion.5
  97.5 1.4 collective-permute-start
  98.9 5.5 %collective-permute-done = bf16[2,128,256]{2,1,0:T(8,128)(2,1)S(1)} collective-permute-done((bf16[2,128,256]{2,1,0:T(8,128)(2,1)S(1)}, bf16[2,128,256]{2,1,0:T(8,128)(2,1)S(1)}, u32[]{:S(2)}, u32[]{:S(2)}) %collective-permute-start) | collective-permute-done | bytes 131104 | tf_op jit(solution)/shard_map/ppermute | solution.py:38
  104.3 5.5 %collective-permute-done.1 = bf16[2,128,256]{2,1,0:T(8,128)(2,1)S(1)} collective-permute-done((bf16[2,128,256]{2,1,0:T(8,128)(2,1)S(1)}, bf16[2,128,256]{2,1,0:T(8,128)(2,1)S(1)}, u32[]{:S(2)}, u32[]{:S(2)}) %collective-permute-start.1) | collective-permute-done | bytes 131104 | tf_op jit(solution)/shard_map/ppermute | solution.py:38
  109.8 5.0 %collective-permute-done.2 = bf16[2,128,256]{2,1,0:T(8,128)(2,1)S(1)} collective-permute-done((bf16[2,128,256]{2,1,0:T(8,128)(2,1)S(1)}, bf16[2,128,256]{2,1,0:T(8,128)(2,1)S(1)}, u32[]{:S(2)}, u32[]{:S(2)}) %collective-permute-start.2) | collective-permute-done | bytes 131104 | tf_op jit(solution)/shard_map/ppermute | solution.py:38
  114.8 5.0 %collective-permute-done.3 = bf16[2,128,256]{2,1,0:T(8,128)(2,1)S(1)} collective-permute-done((bf16[2,128,256]{2,1,0:T(8,128)(2,1)S(1)}, bf16[2,128,256]{2,1,0:T(8,128)(2,1)S(1)}, u32[]{:S(2)}, u32[]{:S(2)}) %collective-permute-start.3) | collective-permute-done | bytes 131104 | tf_op jit(solution)/shard_map/ppermute | solution.py:38
  119.9 5.0 %collective-permute-done.4 = bf16[2,128,256]{2,1,0:T(8,128)(2,1)S(1)} collective-permute-done((bf16[2,128,256]{2,1,0:T(8,128)(2,1)S(1)}, bf16[2,128,256]{2,1,0:T(8,128)(2,1)S(1)}, u32[]{:S(2)}, u32[]{:S(2)}) %collective-permute-start.4) | collective-permute-done | bytes 131104 | tf_op jit(solution)/shard_map/ppermute | solution.py:38
  124.9 5.8 %collective-permute-done.5 = bf16[2,128,256]{2,1,0:T(8,128)(2,1)S(1)} collective-permute-done((bf16[2,128,256]{2,1,0:T(8,128)(2,1)S(1)}, bf16[2,128,256]{2,1,0:T(8,128)(2,1)S(1)}, u32[]{:S(2)}, u32[]{:S(2)}) %collective-permute-start.5) | collective-permute-done | bytes 131104 | tf_op jit(solution)/shard_map/ppermute | solution.py:38
  130.7 6.3 %collective-permute-done.6 = bf16[2,128,256]{2,1,0:T(8,128)(2,1)S(1)} collective-permute-done((bf16[2,128,256]{2,1,0:T(8,128)(2,1)S(1)}, bf16[2,128,256]{2,1,0:T(8,128)(2,1)S(1)}, u32[]{:S(2)}, u32[]{:S(2)}) %collective-permute-start.6) | collective-permute-done | bytes 131104 | tf_op jit(solution)/shard_map/ppermute | solution.py:38
  139.3 1.5 fusion.10
  142.0 119.5 %all-reduce.3.cloned.1.call-done = f32[2,128,1024]{2,1,0:T(8,128)} async-done(((f32[2,128,1024]{2,1,0:T(8,128)}), f32[2,128,1024]{2,1,0:T(8,128)}) %all-reduce.3.cloned.1.call-update) | async-done | bytes 1048592 | tf_op jit(solution)/shard_map/psum | solution.py:55
  261.5 2.0 fusion.43
  263.5 13.7 %psum.53 = f32[2,256]{1,0:T(2,128)S(1)} all-reduce(f32[2,256]{1,0:T(2,128)S(1)} %get-tuple-element.23), channel_id=1, replica_groups=mesh['batch'=8,'col'=32] {'batch'}, use_global_device_ids=true, to_apply=%region_14.15 | all-reduce | flops 512 | bytes 4096 | tf_op jit(solution)/shard_map/psum | solution.py:65
  277.2 2.7 convolution_bitcast_fusion
  280.0 4.3 convolution_bitcast_fusion.1
  288.5 78.4 %psum.52 = f32[]{:T(128)} all-reduce(f32[]{:T(128)S(6)} %add.99), channel_id=1, replica_groups=mesh['batch'=8,'col'=32] {'batch','col'}, use_global_device_ids=true, to_apply=%region_12.13 | all-reduce | flops 1 | bytes 8 | tf_op jit(solution)/shard_map/psum | solution.py:76
  366.9 2.0 reduce-scatter.5.cloned.1.call-done
  368.9 1.0 fusion.40
  369.9 13.4 %all-reduce = (f32[2,128]{1,0:T(2,128)S(1)}, f32[2,128]{1,0:T(2,128)S(1)}) all-reduce(f32[2,128]{1,0:T(2,128)S(1)} %get-tuple-element.8, f32[2,128]{1,0:T(2,128)S(1)} %get-tuple-element.7), channel_id=1, replica_groups=mesh['batch'=8,'col'=32] {'batch'}, use_global_device_ids=true, to_apply=%region_18.19 | all-reduce | flops 512 | bytes 4096 | tf_op jit(solution)/shard_map/psum | solution.py:91
  385.1 42.9 %reduce-scatter.3.cloned.1.call-done = f32[512,256]{1,0:T(8,128)} async-done(((f32[4096,256]{1,0:T(8,128)}), f32[512,256]{1,0:T(8,128)}) %reduce-scatter.3.cloned.1.call-update) | async-done | bytes 524304 | tf_op jit(solution)/shard_map/reduce_scatter | solution.py:84
  (60 shorter events, 8.8 us)
Async XLA Ops:
  7.2 88.0 %copy-start = (bf16[4096,256]{1,0:T(8,128)(2,1)S(1)}, bf16[4096,256]{1,0:T(8,128)(2,1)}, u32[]{:S(2)}) copy-start(bf16[4096,256]{1,0:T(8,128)(2,1)} %param.7) | copy-start | bytes 6291460
  7.2 88.0 %all-gather.2.cloned.1.call-start = ((), (), s32[]{:S(2)}) async-start(), calls=%async_computation.2 | async-start | bytes 2162688 | tf_op jit(solution)/shard_map/all_gather | solution.py:32
  38.8 222.7 %all-reduce.3.cloned.1.call-start = ((), (), s32[]{:S(2)}) async-start(), calls=%async_computation.3 | async-start | bytes 2097152 | tf_op jit(solution)/shard_map/psum | solution.py:55
  97.5 6.8 %collective-permute-start = (bf16[2,128,256]{2,1,0:T(8,128)(2,1)S(1)}, bf16[2,128,256]{2,1,0:T(8,128)(2,1)S(1)}, u32[]{:S(2)}, u32[]{:S(2)}) collective-permute-start(bf16[2,128,256]{2,1,0:T(8,128)(2,1)S(1)} %fusion.5), channel_id=1, source_target_pairs={{0,32},{32,64},{64,96},{96,128},{128,160},{160,192},{192,224},{224... | collective-permute-start | bytes 393224 | tf_op jit(solution)/shard_map/ppermute | solution.py:38
  104.3 5.5 %collective-permute-start.1 = (bf16[2,128,256]{2,1,0:T(8,128)(2,1)S(1)}, bf16[2,128,256]{2,1,0:T(8,128)(2,1)S(1)}, u32[]{:S(2)}, u32[]{:S(2)}) collective-permute-start(bf16[2,128,256]{2,1,0:T(8,128)(2,1)S(1)} %collective-permute-done), channel_id=1, source_target_pairs={{0,32},{32,64},{64,96},{96,128},{128,160},{160,192},{192,224},{224... | collective-permute-start | bytes 393224 | tf_op jit(solution)/shard_map/ppermute | solution.py:38
  109.8 5.0 %collective-permute-start.2 = (bf16[2,128,256]{2,1,0:T(8,128)(2,1)S(1)}, bf16[2,128,256]{2,1,0:T(8,128)(2,1)S(1)}, u32[]{:S(2)}, u32[]{:S(2)}) collective-permute-start(bf16[2,128,256]{2,1,0:T(8,128)(2,1)S(1)} %collective-permute-done.1), channel_id=1, source_target_pairs={{0,32},{32,64},{64,96},{96,128},{128,160},{160,192},{192,224},{224... | collective-permute-start | bytes 393224 | tf_op jit(solution)/shard_map/ppermute | solution.py:38
  114.8 5.0 %collective-permute-start.3 = (bf16[2,128,256]{2,1,0:T(8,128)(2,1)S(1)}, bf16[2,128,256]{2,1,0:T(8,128)(2,1)S(1)}, u32[]{:S(2)}, u32[]{:S(2)}) collective-permute-start(bf16[2,128,256]{2,1,0:T(8,128)(2,1)S(1)} %collective-permute-done.2), channel_id=1, source_target_pairs={{0,32},{32,64},{64,96},{96,128},{128,160},{160,192},{192,224},{224... | collective-permute-start | bytes 393224 | tf_op jit(solution)/shard_map/ppermute | solution.py:38
  119.9 5.0 %collective-permute-start.4 = (bf16[2,128,256]{2,1,0:T(8,128)(2,1)S(1)}, bf16[2,128,256]{2,1,0:T(8,128)(2,1)S(1)}, u32[]{:S(2)}, u32[]{:S(2)}) collective-permute-start(bf16[2,128,256]{2,1,0:T(8,128)(2,1)S(1)} %collective-permute-done.3), channel_id=1, source_target_pairs={{0,32},{32,64},{64,96},{96,128},{128,160},{160,192},{192,224},{224... | collective-permute-start | bytes 393224 | tf_op jit(solution)/shard_map/ppermute | solution.py:38
  124.9 5.8 %collective-permute-start.5 = (bf16[2,128,256]{2,1,0:T(8,128)(2,1)S(1)}, bf16[2,128,256]{2,1,0:T(8,128)(2,1)S(1)}, u32[]{:S(2)}, u32[]{:S(2)}) collective-permute-start(bf16[2,128,256]{2,1,0:T(8,128)(2,1)S(1)} %collective-permute-done.4), channel_id=1, source_target_pairs={{0,32},{32,64},{64,96},{96,128},{128,160},{160,192},{192,224},{224... | collective-permute-start | bytes 393224 | tf_op jit(solution)/shard_map/ppermute | solution.py:38
  130.7 6.3 %collective-permute-start.6 = (bf16[2,128,256]{2,1,0:T(8,128)(2,1)S(1)}, bf16[2,128,256]{2,1,0:T(8,128)(2,1)S(1)}, u32[]{:S(2)}, u32[]{:S(2)}) collective-permute-start(bf16[2,128,256]{2,1,0:T(8,128)(2,1)S(1)} %collective-permute-done.5), channel_id=1, source_target_pairs={{0,32},{32,64},{64,96},{96,128},{128,160},{160,192},{192,224},{224... | collective-permute-start | bytes 393224 | tf_op jit(solution)/shard_map/ppermute | solution.py:38
  137.3 1.3 copy-start.1
  137.8 1.5 copy-start.2
  140.8 228.1 %reduce-scatter.5.cloned.1.call-start = ((), (), s32[]{:S(2)}) async-start(), calls=%async_computation.5 | async-start | bytes 4325376 | tf_op jit(solution)/shard_map/reduce_scatter | solution.py:77
  280.0 148.1 %reduce-scatter.3.cloned.1.call-start = ((), (), s32[]{:S(2)}) async-start(), calls=%async_computation.4 | async-start | bytes 4718592 | tf_op jit(solution)/shard_map/reduce_scatter | solution.py:84
  284.3 2.7 copy-start.4
  284.3 84.6 %copy-start.3 = (bf16[2,128,128]{2,1,0:T(8,128)(2,1)S(1)}, bf16[2,128,128]{2,1,0:T(8,128)(2,1)}, u32[]{:S(2)}) copy-start(bf16[2,128,128]{2,1,0:T(8,128)(2,1)} %param.4) | copy-start | bytes 196612
  284.3 84.6 %copy-start.5 = (f32[128]{0:T(128)S(1)}, f32[128]{0:T(128)}, u32[]{:S(2)}) copy-start(f32[128]{0:T(128)} %param.5) | copy-start | bytes 1540
  284.3 84.6 %copy-start.6 = (f32[128]{0:T(128)S(1)}, f32[128]{0:T(128)}, u32[]{:S(2)}) copy-start(f32[128]{0:T(128)} %param.6) | copy-start | bytes 1540
Sparse Core Ops, SparseCore 0:
  38.9 56.2 all-gather.1
  140.9 120.5 all-reduce.2
  280.1 88.7 reduce-scatter.4
  371.9 56.1 reduce-scatter.2
